TPU v7x, 32 devices: a whole 2x2x4 slice. The times are simulated.
32 devices in a mesh: dp: 4 (over z), expert: 8 (over y, x, core).
Axes of the slice: x: 2, y: 2, z: 4, core: 2. Of those that a mesh axis runs over, the one named last changes fastest.
Arguments:
- tokens: bfloat16 [8192, 1536], P(('dp', 'expert')), may hold values from -6 to 6
- segment_ids: int32 [8192], P('dp'), may hold values from 0 to 7, never falling along the last dimension, each value on 1 to 2048 neighbouring positions
- expert_ids: int32 [8192, 8], P(('dp', 'expert')), may hold values from 0 to 15, all different within a row; in each aligned block of 256 rows (0 to 255, 256 to 511, ...) at most 160 rows name the same one
- w_query: bfloat16 [1536, 1536], P(('dp', 'expert')), may hold values from -0.5 to 0.5
- w_key_value: bfloat16 [1536, 1024], P(('dp', 'expert')), may hold values from -0.5 to 0.5
- w_out: bfloat16 [1536, 1536], P(None, ('dp', 'expert')), may hold values from -1.75 to 1.75
- w_router: bfloat16 [1536, 16], P(('dp', 'expert')), may hold values from -0.078125 to 0.078125
- norm_attn: bfloat16 [1536], P(('dp', 'expert')), may hold values from 0.5 to 1.5
- norm_moe: bfloat16 [1536], P(('dp', 'expert')), may hold values from 0.5 to 1.5
- w_gate_up: bfloat16 [16, 1536, 1024], P('expert'), may hold values from -0.15625 to 0.15625
- w_down: bfloat16 [16, 512, 1536], P('expert'), may hold values from -6 to 6
- grad_out: bfloat16 [8192, 1536], P(('dp', 'expert')), may hold values from -6 to 6
Outputs:
- result: bfloat16 [8192, 1536], P(('dp', 'expert'))
- grad_tokens: bfloat16 [8192, 1536], P(('dp', 'expert'))
- grad_w_query: float32 [1536, 1536], P(('dp', 'expert'))
- grad_w_key_value: float32 [1536, 1024], P(('dp', 'expert'))
- grad_w_out: float32 [1536, 1536], P(None, ('dp', 'expert'))
- grad_w_router: float32 [1536, 16], P(('dp', 'expert'))
- grad_norm_attn: float32 [1536], P(('dp', 'expert'))
- grad_norm_moe: float32 [1536], P(('dp', 'expert'))
- grad_w_gate_up: float32 [16, 1536, 1024], P('expert', 'dp')
- grad_w_down: float32 [16, 512, 1536], P('expert', None, 'dp')
Inputs may be any that keep to these rules, and one draw needn't show every extreme that they name: `expert_ids`: within the 256 tokens of one device a row names 8 different experts, and no expert is named more than 160 times; in every draw some expert is named exactly 160 times by one device's tokens.
All inputs are finite; a program needn't handle non-finite values.
Results may differ from a plain program's by a relative error of at most 0.02.
Values may be sent and summed in bfloat16 or wider, within the bound.
No kernel may reach another device: no remote copies, remote signals or barrier semaphores. Data moves between devices by JAX's collectives and lax.ppermute only.
A program may use at most 256 MiB of HBM per device.

v0:
```python
import jax
import jax.numpy as jnp
from jax import lax
from jax.sharding import PartitionSpec as P

D = 1536
HEADS = 24
KV_HEADS = 8
HEAD_DIM = 64
FF = 512
TOP = 8
EXP_DEV = 2
SEQ_MIN = 1024
RESIDUAL = 0.22
ATTN_SCALE = 0.015625
EPSILON = 1e-06
ROPE_BASE = 10000.0
MASKED = -1e30


def rms_scale(values, gain_vec):
    return (
        values * lax.rsqrt(jnp.mean(values * values, axis=-1, keepdims=True) + EPSILON) * gain_vec
    )


def rope_tables(position):
    half_dim = HEAD_DIM // 2
    frequency = ROPE_BASE ** (-(jnp.arange(half_dim, dtype=jnp.float32) * 2.0 / HEAD_DIM))
    angles = position.astype(jnp.float32)[:, None] * frequency[None, :]
    return (jnp.cos(angles), jnp.sin(angles))


def rotate(flat_rows, cosine, sine_table):
    row_count = flat_rows.shape[0]
    pieces = flat_rows.reshape(row_count, -1, HEAD_DIM)
    half_dim = HEAD_DIM // 2
    first_half = pieces[..., :half_dim]
    second_half = pieces[..., half_dim:]
    cos_part = cosine[:, None, :]
    sin_part = sine_table[:, None, :]
    turned = jnp.concatenate(
        [
            first_half * cos_part - second_half * sin_part,
            second_half * cos_part + first_half * sin_part,
        ],
        axis=-1,
    )
    return turned.reshape(row_count, -1)


def slot_index(route_flat, expert_total, capacity):
    one_hot = (route_flat[:, None] == jnp.arange(expert_total, dtype=jnp.int32)).astype(jnp.int32)
    rank_table = jnp.cumsum(one_hot, axis=0) - 1
    slot_number = jnp.sum(rank_table * one_hot, axis=-1)
    return route_flat * capacity + slot_number


def split_heads(pair_rows):
    pair_width = KV_HEADS * HEAD_DIM
    key_heads = jnp.moveaxis(pair_rows[:, :pair_width].reshape(-1, KV_HEADS, HEAD_DIM), 1, 0)
    value_heads = jnp.moveaxis(pair_rows[:, pair_width:].reshape(-1, KV_HEADS, HEAD_DIM), 1, 0)
    return (key_heads, value_heads)


def shards(
    tokens,
    segment_ids,
    expert_ids,
    w_query,
    w_key_value,
    w_out,
    w_router,
    norm_attn,
    norm_moe,
    w_gate_up,
    w_down,
    grad_out,
):
    full_query, full_pair, full_out, full_router, gain_attn, gain_moe = (
        lax.all_gather(w_query, ("dp", "expert"), axis=0, tiled=True),
        lax.all_gather(w_key_value, ("dp", "expert"), axis=0, tiled=True),
        lax.all_gather(w_out, ("dp", "expert"), axis=1, tiled=True),
        lax.all_gather(w_router, ("dp", "expert"), axis=0, tiled=True),
        lax.all_gather(norm_attn, ("dp", "expert"), axis=0, tiled=True),
        lax.all_gather(norm_moe, ("dp", "expert"), axis=0, tiled=True),
    )
    gain_attn = gain_attn.astype(jnp.float32)
    gain_moe = gain_moe.astype(jnp.float32)
    tok_rows = tokens.shape[0]
    members = lax.axis_size("expert")
    position = lax.axis_index("expert")
    seq_length = max(SEQ_MIN, tok_rows * members)
    expert_total = EXP_DEV * members
    capacity = min(tok_rows, 5 * tok_rows * TOP // (4 * expert_total))
    pair_width = KV_HEADS * HEAD_DIM
    group_size = HEADS // KV_HEADS
    query_pos = position * tok_rows + jnp.arange(tok_rows, dtype=jnp.int32)
    key_start = position * tok_rows // seq_length * seq_length
    key_pos = key_start + jnp.arange(seq_length, dtype=jnp.int32)
    query_seg = lax.dynamic_slice_in_dim(segment_ids, position * tok_rows, tok_rows, 0)
    allowed = (query_seg[:, None] == segment_ids[None, :]) & (
        query_pos[:, None] >= key_pos[None, :]
    )
    cosine, sine_table = rope_tables(query_pos % seq_length)
    tokens_f = tokens.astype(jnp.float32)
    normed = rms_scale(tokens_f, gain_attn).astype(jnp.bfloat16)
    queries = jnp.dot(normed, full_query, preferred_element_type=jnp.float32)
    key_value = jnp.dot(normed, full_pair, preferred_element_type=jnp.float32)
    queries_low = rotate(queries, cosine, sine_table).astype(jnp.bfloat16)
    pair_low = jnp.concatenate(
        [rotate(key_value[:, :pair_width], cosine, sine_table), key_value[:, pair_width:]], axis=1
    ).astype(jnp.bfloat16)
    pair_group = lax.all_gather(pair_low, "expert", axis=0, tiled=True)
    query_heads = jnp.moveaxis(queries_low.reshape(tok_rows, KV_HEADS, group_size, HEAD_DIM), 1, 0)
    key_heads, value_heads = split_heads(pair_group)

    def head_probs(query_head, key_head):
        raw_scores = jnp.einsum(
            "qgd,kd->gqk", query_head, key_head, preferred_element_type=jnp.float32
        )
        scores = jnp.where(allowed[None], raw_scores * ATTN_SCALE, MASKED)
        largest = jnp.max(scores, axis=-1, keepdims=True)
        exponent = jnp.exp(scores - largest)
        return exponent / jnp.sum(exponent, axis=-1, keepdims=True)

    def head_forward(operands):
        query_head, key_head, value_head = operands
        probability = head_probs(query_head, key_head)
        return jnp.einsum(
            "gqk,kd->qgd",
            probability.astype(jnp.bfloat16),
            value_head,
            preferred_element_type=jnp.float32,
        )

    attended = lax.map(head_forward, (query_heads, key_heads, value_heads))
    mixed_low = (
        jnp.moveaxis(attended, 0, 1).reshape(tok_rows, HEADS * HEAD_DIM).astype(jnp.bfloat16)
    )
    after_attn = tokens_f + RESIDUAL * jnp.dot(
        mixed_low, full_out, preferred_element_type=jnp.float32
    )
    normed_moe = rms_scale(after_attn, gain_moe).astype(jnp.bfloat16)
    logits = jnp.dot(normed_moe, full_router, preferred_element_type=jnp.float32)
    one_hot = (expert_ids[:, :, None] == jnp.arange(expert_total, dtype=jnp.int32)).astype(
        jnp.float32
    )
    chosen = jnp.sum(one_hot * logits[:, None, :], axis=-1)
    gate_weights = jax.nn.softmax(chosen, axis=-1)
    targets = slot_index(expert_ids.reshape(-1), expert_total, capacity)
    routed = jnp.repeat(normed_moe, TOP, axis=0)
    send_rows = (
        jnp.zeros((expert_total * capacity, D), jnp.bfloat16)
        .at[targets]
        .set(routed)
        .reshape(members, EXP_DEV * capacity, D)
    )
    arrived = lax.all_to_all(send_rows, "expert", split_axis=0, concat_axis=0, tiled=True).reshape(
        members, EXP_DEV, capacity, D
    )
    gate_up = jnp.einsum("secd,edf->secf", arrived, w_gate_up, preferred_element_type=jnp.float32)
    gate_part = gate_up[..., :FF]
    up_part = gate_up[..., FF:]
    activated = (jax.nn.silu(gate_part) * up_part).astype(jnp.bfloat16)
    expert_out = jnp.einsum(
        "secf,efd->secd", activated, w_down, preferred_element_type=jnp.float32
    ).astype(jnp.bfloat16)
    replies = lax.all_to_all(
        expert_out.reshape(members, EXP_DEV * capacity, D),
        "expert",
        split_axis=0,
        concat_axis=0,
        tiled=True,
    ).reshape(expert_total * capacity, D)
    returned_f = replies[targets].reshape(tok_rows, TOP, D).astype(jnp.float32)
    combined = jnp.sum(gate_weights[:, :, None] * returned_f, axis=1)
    result = (after_attn + RESIDUAL * combined).astype(jnp.bfloat16)
    grad_final = grad_out.astype(jnp.float32)
    gate_grads = RESIDUAL * jnp.sum(returned_f * grad_final[:, None, :], axis=-1)
    out_grads = (
        (gate_weights[:, :, None] * (RESIDUAL * grad_final)[:, None, :])
        .astype(jnp.bfloat16)
        .reshape(tok_rows * TOP, D)
    )
    send_grads = (
        jnp.zeros((expert_total * capacity, D), jnp.bfloat16)
        .at[targets]
        .set(out_grads)
        .reshape(members, EXP_DEV * capacity, D)
    )
    arrived_grads = lax.all_to_all(
        send_grads, "expert", split_axis=0, concat_axis=0, tiled=True
    ).reshape(members, EXP_DEV, capacity, D)
    act_grads = jnp.einsum(
        "secd,efd->secf", arrived_grads, w_down, preferred_element_type=jnp.float32
    )
    down_wgrads = jnp.einsum(
        "secf,secd->efd", activated, arrived_grads, preferred_element_type=jnp.float32
    )
    sigmoid_gate = jax.nn.sigmoid(gate_part)
    grad_gate = act_grads * up_part * sigmoid_gate * (1.0 + gate_part * (1.0 - sigmoid_gate))
    grad_up = act_grads * jax.nn.silu(gate_part)
    gate_up_low = jnp.concatenate([grad_gate, grad_up], axis=-1).astype(jnp.bfloat16)
    gate_up_wgrads = jnp.einsum(
        "secd,secf->edf", arrived, gate_up_low, preferred_element_type=jnp.float32
    )
    input_rows = jnp.einsum(
        "secf,edf->secd", gate_up_low, w_gate_up, preferred_element_type=jnp.float32
    ).astype(jnp.bfloat16)
    back_rows = lax.all_to_all(
        input_rows.reshape(members, EXP_DEV * capacity, D),
        "expert",
        split_axis=0,
        concat_axis=0,
        tiled=True,
    ).reshape(expert_total * capacity, D)
    moe_input_grad = jnp.sum(
        back_rows[targets].reshape(tok_rows, TOP, D).astype(jnp.float32), axis=1
    )
    chosen_grads = gate_weights * (
        gate_grads - jnp.sum(gate_weights * gate_grads, axis=-1, keepdims=True)
    )
    logit_grads = jnp.sum(one_hot * chosen_grads[:, :, None], axis=1).astype(jnp.bfloat16)
    router_wgrad = jnp.dot(normed_moe.T, logit_grads, preferred_element_type=jnp.float32)
    normed_moe_grad = moe_input_grad + jnp.dot(
        logit_grads, full_router.T, preferred_element_type=jnp.float32
    )
    unused_moe, moe_pull = jax.vjp(rms_scale, after_attn, gain_moe)
    attn_out_grad, moe_gain_grad = moe_pull(normed_moe_grad)
    resid_grad = grad_final + attn_out_grad
    branch_grad = (RESIDUAL * resid_grad).astype(jnp.bfloat16)
    out_wgrad = jnp.dot(mixed_low.T, branch_grad, preferred_element_type=jnp.float32)
    mixed_grad = jnp.dot(branch_grad, full_out.T, preferred_element_type=jnp.float32).astype(
        jnp.bfloat16
    )
    mixed_heads = jnp.moveaxis(mixed_grad.reshape(tok_rows, KV_HEADS, group_size, HEAD_DIM), 1, 0)
    key_back, value_back = (key_heads, value_heads)

    def head_backward(operands):
        query_head, key_head, value_head, out_grad = operands
        probability = head_probs(query_head, key_head)
        value_grad = jnp.einsum(
            "gqk,qgd->kd",
            probability.astype(jnp.bfloat16),
            out_grad,
            preferred_element_type=jnp.float32,
        )
        prob_grad = jnp.einsum(
            "qgd,kd->gqk", out_grad, value_head, preferred_element_type=jnp.float32
        )
        score_grad = (
            probability
            * (prob_grad - jnp.sum(probability * prob_grad, axis=-1, keepdims=True))
            * ATTN_SCALE
        ).astype(jnp.bfloat16)
        query_grad = jnp.einsum(
            "gqk,kd->qgd", score_grad, key_head, preferred_element_type=jnp.float32
        )
        key_grad = jnp.einsum(
            "gqk,qgd->kd", score_grad, query_head, preferred_element_type=jnp.float32
        )
        return (query_grad, key_grad, value_grad)

    query_grads, key_grads, value_grads = lax.map(
        head_backward, (query_heads, key_back, value_back, mixed_heads)
    )
    query_grad = jnp.moveaxis(query_grads, 0, 1).reshape(tok_rows, HEADS * HEAD_DIM)
    pair_grad_seq = jnp.concatenate(
        [
            jnp.moveaxis(key_grads, 0, 1).reshape(seq_length, pair_width),
            jnp.moveaxis(value_grads, 0, 1).reshape(seq_length, pair_width),
        ],
        axis=1,
    )
    pair_grad = lax.psum_scatter(
        pair_grad_seq.astype(jnp.bfloat16), "expert", scatter_dimension=0, tiled=True
    ).astype(jnp.float32)
    query_grad_low = rotate(query_grad, cosine, -sine_table).astype(jnp.bfloat16)
    pair_grad_low = jnp.concatenate(
        [rotate(pair_grad[:, :pair_width], cosine, -sine_table), pair_grad[:, pair_width:]], axis=1
    ).astype(jnp.bfloat16)
    query_wgrad = jnp.dot(normed.T, query_grad_low, preferred_element_type=jnp.float32)
    pair_wgrad = jnp.dot(normed.T, pair_grad_low, preferred_element_type=jnp.float32)
    normed_grad = jnp.dot(
        query_grad_low, full_query.T, preferred_element_type=jnp.float32
    ) + jnp.dot(pair_grad_low, full_pair.T, preferred_element_type=jnp.float32)
    unused_attn, attn_pull = jax.vjp(rms_scale, tokens_f, gain_attn)
    token_norm_grad, attn_gain_grad = attn_pull(normed_grad)
    token_grad = (resid_grad + token_norm_grad).astype(jnp.bfloat16)
    shared = (
        lax.psum_scatter(query_wgrad, ("dp", "expert"), scatter_dimension=0, tiled=True),
        lax.psum_scatter(pair_wgrad, ("dp", "expert"), scatter_dimension=0, tiled=True),
        lax.psum_scatter(out_wgrad, ("dp", "expert"), scatter_dimension=1, tiled=True),
        lax.psum_scatter(router_wgrad, ("dp", "expert"), scatter_dimension=0, tiled=True),
        lax.psum_scatter(attn_gain_grad, ("dp", "expert"), scatter_dimension=0, tiled=True),
        lax.psum_scatter(moe_gain_grad, ("dp", "expert"), scatter_dimension=0, tiled=True),
    )
    gate_up_share, down_share = (
        lax.psum_scatter(
            gate_up_wgrads.astype(jnp.bfloat16), "dp", scatter_dimension=1, tiled=True
        ).astype(jnp.float32),
        lax.psum_scatter(
            down_wgrads.astype(jnp.bfloat16), "dp", scatter_dimension=2, tiled=True
        ).astype(jnp.float32),
    )
    return (
        result,
        token_grad,
        shared[0],
        shared[1],
        shared[2],
        shared[3],
        shared[4],
        shared[5],
        gate_up_share,
        down_share,
    )


def solution(mesh):
    in_specs = (
        P(("dp", "expert"), None),
        P("dp"),
        P(("dp", "expert"), None),
        P(("dp", "expert"), None),
        P(("dp", "expert"), None),
        P(None, ("dp", "expert")),
        P(("dp", "expert"), None),
        P(("dp", "expert")),
        P(("dp", "expert")),
        P("expert", None, None),
        P("expert", None, None),
        P(("dp", "expert"), None),
    )
    out_specs = (
        P(("dp", "expert"), None),
        P(("dp", "expert"), None),
        P(("dp", "expert"), None),
        P(("dp", "expert"), None),
        P(None, ("dp", "expert")),
        P(("dp", "expert"), None),
        P(("dp", "expert")),
        P(("dp", "expert")),
        P("expert", "dp", None),
        P("expert", None, "dp"),
    )
    return jax.shard_map(shards, mesh=mesh, in_specs=in_specs, out_specs=out_specs, check_vma=False)
```

profile of v0, /device:TPU:0, one launch (start us, length us, event | category | flops | bytes accessed | tf_op | source)
XLA Modules:
  0.0 1843.8 jit_solution(649643439071911868)
XLA Ops:
  10.4 42.1 %all-reduce.5 = (bf16[1536]{0:T(1024)(128)(2,1)S(1)}, bf16[1536]{0:T(1024)(128)(2,1)S(1)}) all-reduce(bf16[1536]{0:T(1024)(128)(2,1)S(1)} %dynamic-update-slice, bf16[1536]{0:T(1024)(128)(2,1)S(1)} %dynamic-update-slice.1), channel_id=1, replica_groups=mesh['dp'=4,'expert'=8] {'dp','expert'}, use_global_device_ids=true, to_apply=%add | all-reduce | flops 3072 | bytes 12288
  54.8 17.8 all-gather.6.cloned.1.call-done
  96.7 41.3 %all-gather.10.cloned.1.call-done = bf16[1536,1536]{1,0:T(8,128)(2,1)} async-done(((bf16[48,1536]{1,0:T(8,128)(2,1)}), bf16[1536,1536]{1,0:T(8,128)(2,1)}) %all-gather.10.cloned.1.call-update) | async-done | bytes 4718608 | tf_op jit(solution)/shard_map/all_gather | solution.py:81
  143.9 32.2 %all-gather.8.cloned.1.call-done = bf16[2048,1024]{1,0:T(8,128)(2,1)} async-done(((bf16[256,1024]{1,0:T(8,128)(2,1)}), bf16[2048,1024]{1,0:T(8,128)(2,1)}) %all-gather.8.cloned.1.call-update) | async-done | bytes 4194320 | tf_op jit(solution)/shard_map/all_gather | solution.py:114
  188.5 100.8 %while.28 = (s32[]{:T(128)}, bf16[8,256,3,64]{1,3,2,0:T(8,128)(2,1)}, bf16[8,2048,64]{1,2,0:T(8,128)(2,1)}, bf16[8,2048,64]{1,2,0:T(8,128)(2,1)}, bf16[8,256,3,6...) while((s32[]{:T(128)}, ...), condition=%wide.region_4.5_spmd.clone.clone, body=%wide.region_1.4_spmd.clone.sunk.clone | while | flops 413665280 | bytes 14477405 | solution.py:137
  295.9 15.1 scatter_custom_fusion
  316.0 120.6 %all-gather = bf16[32,48,16]{1,2,0:T(8,128)(2,1)S(1)} all-gather(bf16[1,48,16]{1,2,0:T(8,128)(2,1)S(1)} %bitcast.376), channel_id=1, replica_groups=mesh['dp'=4,'expert'=8] {'dp','expert'}, dimensions={0}, use_global_device_ids=true | all-gather | bytes 50688 | tf_op jit(solution)/shard_map/all_gather | solution.py:84
  441.1 15.8 scatter_custom_fusion.1
  461.9 14.9 fusion.142
  476.8 73.5 %all-to-all-done.2 = bf16[8,320,1536]{2,1,0:T(8,128)(2,1)} async-done(((bf16[8,320,1536]{2,1,0:T(8,128)(2,1)}), bf16[8,320,1536]{2,1,0:T(8,128)(2,1)}, u32[]{:S(2)}, u32[]{:S(2)}) %all-to-all-start.2) | async-done | bytes 7864352 | tf_op jit(solution)/shard_map/all_to_all | solution.py:192
  583.1 13.7 convert_bitcast_fusion
  603.9 67.7 %all-to-all-done.1 = bf16[8,320,1536]{2,1,0:T(8,128)(2,1)} async-done(((bf16[8,320,1536]{2,1,0:T(8,128)(2,1)}), bf16[8,320,1536]{2,1,0:T(8,128)(2,1)}, u32[]{:S(2)}, u32[]{:S(2)}) %all-to-all-start.1) | async-done | bytes 7864352 | tf_op jit(solution)/shard_map/all_to_all | solution.py:169
  677.1 17.5 gather_fusion
  704.3 61.0 %all-to-all-done.3 = bf16[8,320,1536]{2,1,0:T(8,128)(2,1)} async-done(((bf16[8,320,1536]{2,1,0:T(8,128)(2,1)}), bf16[8,320,1536]{2,1,0:T(8,128)(2,1)}, u32[]{:S(2)}, u32[]{:S(2)}) %all-to-all-start.3) | async-done | bytes 7864352 | tf_op jit(solution)/shard_map/all_to_all | solution.py:211
  765.3 17.5 gather_fusion.1
  794.7 307.4 %while.29 = (s32[]{:T(128)}, f32[8,256,3,64]{1,3,2,0:T(8,128)}, bf16[8,2048,64]{1,2,0:T(8,128)(2,1)}, bf16[8,2048,64]{1,2,0:T(8,128)(2,1)}, bf16[8,2048,64]{1,2,...) while((s32[]{:T(128)}, f32[8,256,3,64]{1,3,2,0:T(8,128)}, ...), condition=%wide.region_24.25_spmd.clone.clone, body=%wide.region_20.24_spmd.clone.sunk.clone | while | flops 1039670784 | bytes 72726648 | solution.py:265
  1130.3 14.0 bitcast_convert_fusion
  1163.4 54.6 %reduce-scatter.24.cloned.1.call-done = bf16[384,1024]{1,0:T(8,128)(2,1)} async-done(((bf16[1536,1024]{1,0:T(8,128)(2,1)}), bf16[384,1024]{1,0:T(8,128)(2,1)}) %reduce-scatter.24.cloned.1.call-update) | async-done | bytes 786448
  1227.5 92.0 %reduce-scatter.22.cloned.1.call-done = f32[48,16]{1,0:T(8,128)} async-done(((f32[1536,16]{1,0:T(8,128)}), f32[48,16]{1,0:T(8,128)}) %reduce-scatter.22.cloned.1.call-update) | async-done | bytes 3088
  1320.9 110.8 %reduce-scatter.20.cloned.1.call-done = bf16[2,384,1024]{2,1,0:T(8,128)(2,1)} async-done(((bf16[2,1536,1024]{2,1,0:T(8,128)(2,1)}), bf16[2,384,1024]{2,1,0:T(8,128)(2,1)}) %reduce-scatter.20.cloned.1.call-update) | async-done | bytes 1572880 | tf_op jit(solution)/shard_map/reduce_scatter | solution.py:300
  1440.0 40.9 %all-reduce.4 = (f32[1536]{0:T(1024)S(1)}, f32[1536]{0:T(1024)S(1)}) all-reduce(f32[1536]{0:T(1024)S(1)} %get-tuple-element.153, f32[1536]{0:T(1024)S(1)} %copy-done.25), channel_id=7, replica_groups=mesh['dp'=4,'expert'=8] {'dp','expert'}, use_global_device_ids=true, to_apply=%region_32.33.clone | all-reduce | flops 3072 | bytes 24576
  1485.6 89.8 %reduce-scatter.18.cloned.1.call-done = f32[1536,48]{0,1:T(8,128)} async-done(((f32[1536,1536]{0,1:T(8,128)}), f32[1536,48]{0,1:T(8,128)}) %reduce-scatter.18.cloned.1.call-update) | async-done | bytes 294928 | tf_op jit(solution)/shard_map/reduce_scatter | solution.py:294
  1575.3 140.8 %reduce-scatter.14.cloned.1.call-done = f32[48,1536]{1,0:T(8,128)} async-done(((f32[1536,1536]{1,0:T(8,128)}), f32[48,1536]{1,0:T(8,128)}) %reduce-scatter.14.cloned.1.call-update) | async-done | bytes 294928 | tf_op jit(solution)/shard_map/reduce_scatter | solution.py:292
  1716.2 120.9 %reduce-scatter.16.cloned.1.call-done = f32[48,1024]{1,0:T(8,128)} async-done(((f32[1536,1024]{1,0:T(8,128)}), f32[48,1024]{1,0:T(8,128)}) %reduce-scatter.16.cloned.1.call-update) | async-done | bytes 196624 | tf_op jit(solution)/shard_map/reduce_scatter | solution.py:293
  (271 shorter events, 614.2 us)
Async XLA Ops:
  7.2 543.1 %copy-start = (bf16[2,512,1536]{2,1,0:T(8,128)(2,1)S(1)}, bf16[2,512,1536]{2,1,0:T(8,128)(2,1)}, u32[]{:S(2)}) copy-start(bf16[2,512,1536]{2,1,0:T(8,128)(2,1)} %param.26) | copy-start | bytes 9437188
  7.2 65.4 %all-gather.6.cloned.1.call-start = ((), (), s32[]{:S(2)}) async-start(), calls=%async_computation.11 | async-start | bytes 3244032 | tf_op jit(solution)/shard_map/all_gather | solution.py:82
  7.9 130.1 %all-gather.10.cloned.1.call-start = ((), (), s32[]{:S(2)}) async-start(), calls=%async_computation.13 | async-start | bytes 4866048 | tf_op jit(solution)/shard_map/all_gather | solution.py:81
  8.7 167.4 %all-gather.8.cloned.1.call-start = ((), (), s32[]{:S(2)}) async-start(), calls=%async_computation.12 | async-start | bytes 4718592 | tf_op jit(solution)/shard_map/all_gather | solution.py:114
  52.5 85.5 %copy-start.18 = (f32[1536]{0:T(1024)}, f32[1536]{0:T(1024)S(1)}, u32[]{:S(2)}) copy-start(f32[1536]{0:T(1024)S(1)} %convert_element_type.126) | copy-start | bytes 18436
  53.9 21.8 %copy-start.26 = (f32[256]{0:T(256)}, f32[256]{0:T(256)S(1)}, u32[]{:S(2)}) copy-start(f32[256]{0:T(256)S(1)} %fusion.157) | copy-start | bytes 3076
  53.9 84.1 %copy-start.23 = (f32[256]{0:T(256)}, f32[256]{0:T(256)S(1)}, u32[]{:S(2)}) copy-start(f32[256]{0:T(256)S(1)} %fusion.172) | copy-start | bytes 3076
  54.8 87.9 %copy-start.15 = (f32[256,32]{0,1:T(8,128)}, f32[256,32]{0,1:T(8,128)S(1)}, u32[]{:S(2)}) copy-start(f32[256,32]{0,1:T(8,128)S(1)} %get-tuple-element.224) | copy-start | bytes 98308
  79.4 16.2 copy-start.14
  83.3 206.0 %all-gather.12.cloned.1.call-start = ((), (), s32[]{:S(2)}) async-start(), calls=%async_computation.14 | async-start | bytes 4866048 | tf_op jit(solution)/shard_map/all_gather | solution.py:83
  311.0 146.0 %all-to-all-start = ((bf16[8,320,1536]{2,1,0:T(8,128)(2,1)}), bf16[8,320,1536]{2,1,0:T(8,128)(2,1)}, u32[]{:S(2)}, u32[]{:S(2)}) async-start(bf16[8,320,1536]{2,1,0:T(8,128)(2,1)} %bitcast.347), calls=%async_computation | async-start | bytes 15728640 | tf_op jit(solution)/shard_map/all_to_all | solution.py:159
  457.0 93.3 %all-to-all-start.2 = ((bf16[8,320,1536]{2,1,0:T(8,128)(2,1)}), bf16[8,320,1536]{2,1,0:T(8,128)(2,1)}, u32[]{:S(2)}, u32[]{:S(2)}) async-start(bf16[8,320,1536]{2,1,0:T(8,128)(2,1)} %bitcast.348), calls=%async_computation.2 | async-start | bytes 15728640 | tf_op jit(solution)/shard_map/all_to_all | solution.py:192
  578.0 93.6 %all-to-all-start.1 = ((bf16[8,320,1536]{2,1,0:T(8,128)(2,1)}), bf16[8,320,1536]{2,1,0:T(8,128)(2,1)}, u32[]{:S(2)}, u32[]{:S(2)}) async-start(bf16[8,320,1536]{2,1,0:T(8,128)(2,1)} %bitcast.349), calls=%async_computation.1 | async-start | bytes 15728640 | tf_op jit(solution)/shard_map/all_to_all | solution.py:169
  671.6 93.7 %all-to-all-start.3 = ((bf16[8,320,1536]{2,1,0:T(8,128)(2,1)}), bf16[8,320,1536]{2,1,0:T(8,128)(2,1)}, u32[]{:S(2)}, u32[]{:S(2)}) async-start(bf16[8,320,1536]{2,1,0:T(8,128)(2,1)} %bitcast.346), calls=%async_computation.3 | async-start | bytes 15728640 | tf_op jit(solution)/shard_map/all_to_all | solution.py:211
  676.8 481.4 %reduce-scatter.12.cloned.1.call-start = ((), (), s32[]{:S(2)}) async-start(), calls=%async_computation.15 | async-start | bytes 4718592 | tf_op jit(solution)/shard_map/reduce_scatter | solution.py:276
  704.3 85.6 %copy-start.21 = (bf16[256,16]{0,1:T(8,128)(2,1)}, bf16[256,16]{0,1:T(8,128)(2,1)S(1)}, u32[]{:S(2)}) copy-start(bf16[256,16]{0,1:T(8,128)(2,1)S(1)} %select_reduce_fusion) | copy-start | bytes 24580
  1107.0 111.0 %reduce-scatter.24.cloned.1.call-start = ((), (), s32[]{:S(2)}) async-start(), calls=%async_computation.21 | async-start | bytes 3932160
  1127.8 191.7 %reduce-scatter.22.cloned.1.call-start = ((), (), s32[]{:S(2)}) async-start(), calls=%async_computation.20 | async-start | bytes 811008
  1130.3 301.4 %reduce-scatter.20.cloned.1.call-start = ((), (), s32[]{:S(2)}) async-start(), calls=%async_computation.19 | async-start | bytes 7864320 | tf_op jit(solution)/shard_map/reduce_scatter | solution.py:300
  1144.4 431.0 %reduce-scatter.18.cloned.1.call-start = ((), (), s32[]{:S(2)}) async-start(), calls=%async_computation.18 | async-start | bytes 9732096 | tf_op jit(solution)/shard_map/reduce_scatter | solution.py:294
  1151.1 565.1 %reduce-scatter.14.cloned.1.call-start = ((), (), s32[]{:S(2)}) async-start(), calls=%async_computation.16 | async-start | bytes 9732096 | tf_op jit(solution)/shard_map/reduce_scatter | solution.py:292
  1158.0 679.0 %reduce-scatter.16.cloned.1.call-start = ((), (), s32[]{:S(2)}) async-start(), calls=%async_computation.17 | async-start | bytes 6488064 | tf_op jit(solution)/shard_map/reduce_scatter | solution.py:293
  1435.3 46.8 %copy-start.27 = (f32[256]{0:T(256)S(1)}, f32[256]{0:T(256)}, u32[]{:S(2)}) copy-start(f32[256]{0:T(256)} %copy-done.26) | copy-start | bytes 3076
  1435.3 401.7 %copy-start.1 = (bf16[2,512,1536]{2,1,0:T(8,128)(2,1)S(1)}, bf16[2,512,1536]{2,1,0:T(8,128)(2,1)}, u32[]{:S(2)}) copy-start(bf16[2,512,1536]{2,1,0:T(8,128)(2,1)} %param.26) | copy-start | bytes 9437188
  (26 other events, 79.7 us)
Sparse Core Ops, SparseCore 0:
  10.9 61.6 all-gather.5
  75.5 62.4 all-gather.9
  140.5 35.5 all-gather.7
  178.8 63.6 all-gather.11
  1107.2 47.6 reduce-scatter.11
  1157.7 60.2 reduce-scatter.23
  1223.9 95.5 reduce-scatter.21
  1321.9 109.8 reduce-scatter.19
  1439.2 136.1 reduce-scatter.17
  1581.7 134.4 reduce-scatter.13
  1723.3 113.6 reduce-scatter.15
where the time goes:
time: 1850 us; the launch traced here: 1840 us
  waiting for transfers between devices  904 us (49%)
  matrix products  491 us (27%)
  blocking collectives  204 us (11%)
  local copies, waits for them, and re-layouts  109 us (6%)
  other arithmetic  98.9 us (5%)
  starting transfers between devices  21.5 us (1%)
    unnamed x13, waiting for transfers between devices  148 us
    reduce_scatter x1, waiting for transfers between devices, shards(): lax.psum_scatter(query_wgrad, ('dp', 'expert'), scatter_dimension=0, tile...  141 us
    reduce_scatter x1, waiting for transfers between devices, shards(): lax.psum_scatter(pair_wgrad, ('dp', 'expert'), scatter_dimension=0, tiled...  121 us
    all_gather x1, blocking collectives, shards(): lax.all_gather(w_router, ('dp', 'expert'), axis=0, tiled=True)  121 us
    reduce_scatter x1, waiting for transfers between devices, shards(): lax.psum_scatter(gate_up_wgrads.astype(jnp.bfloat16), 'dp', scatter_dimen...  111 us
    sub x16, matrix products, head_probs(): exponent = jnp.exp(scores - largest)  95.9 us
    reduce_scatter x1, waiting for transfers between devices, shards(): lax.psum_scatter(out_wgrad, ('dp', 'expert'), scatter_dimension=1, tiled=...  89.8 us
    dot_general x8, matrix products, head_backward(): jnp.einsum('gqk,kd->qgd', score_grad, key_head, preferred_element_type=jn...  87.6 us
  transfers between devices with their start and end apart: 15, of which 12 were waited for; matrix products, arithmetic and copies ran while one was open for 16% of the time, Pallas kernels for 0%

commit v1 on v0

--- a/solution.py
+++ b/solution.py
@@ -16,6 +16,29 @@
 EPSILON = 1e-06
 ROPE_BASE = 10000.0
 MASKED = -1e30
+
+
+def in_blocks(x, dim, size):
+    dims = x.shape
+    tiles = x.reshape(*dims[:dim], size, dims[dim] // size, *dims[dim + 1 :])
+    return jnp.moveaxis(tiles, dim, 0)
+
+
+def joined_along(tiles, dim):
+    tiles = jnp.moveaxis(tiles, 0, dim)
+    lengths = tiles.shape
+    return tiles.reshape(*lengths[:dim], lengths[dim] * lengths[dim + 1], *lengths[dim + 2 :])
+
+
+def exchange_in_pairs(x, axis, split_dim, concat_dim):
+    peers, mine = (lax.axis_size(axis), lax.axis_index(axis))
+    pieces = in_blocks(x, split_dim, peers)
+    done = [pieces[mine]]
+    for turn in range(1, peers):
+        sent = pieces[mine ^ turn]
+        done.append(lax.ppermute(sent, axis, [(i, i ^ turn) for i in range(peers)]))
+    pieces = jnp.stack(done)[mine ^ jnp.arange(peers)]
+    return joined_along(pieces, concat_dim)
 
 
 def rms_scale(values, gain_vec):
@@ -166,12 +189,8 @@
     expert_out = jnp.einsum(
         "secf,efd->secd", activated, w_down, preferred_element_type=jnp.float32
     ).astype(jnp.bfloat16)
-    replies = lax.all_to_all(
-        expert_out.reshape(members, EXP_DEV * capacity, D),
-        "expert",
-        split_axis=0,
-        concat_axis=0,
-        tiled=True,
+    replies = exchange_in_pairs(
+        expert_out.reshape(members, EXP_DEV * capacity, D), "expert", 0, 0
     ).reshape(expert_total * capacity, D)
     returned_f = replies[targets].reshape(tok_rows, TOP, D).astype(jnp.float32)
     combined = jnp.sum(gate_weights[:, :, None] * returned_f, axis=1)

time: 1850 us -> 1890 us (1.022)
  local copies, waits for them, and re-layouts: 109 us -> 132 us
    ppermute x0 -> x7, waiting for transfers between devices: none -> 137 us  [exchange_in_pairs(): done.append(lax.ppermute(sent, axis, [(i, i ^ turn) for i in range(peers)]))]
    all_to_all x1 -> x0, waiting for transfers between devices: 67.7 us -> none  [shards(): lax.all_to_all(expert_out.reshape(members, EXP_DEV * capacity, D), 'exper...]
    all_to_all x1, waiting for transfers between devices: 61 us -> 0.01 us  [shards(): lax.all_to_all(input_rows.reshape(members, EXP_DEV * capacity, D), 'exper...]
  transfers between devices with their start and end apart: 15 -> 21, of which waited for: 12 -> 13; matrix products, arithmetic and copies ran while one was open for 16% -> 17% of each run, Pallas kernels for 0% -> 0%
where the time goes in v1:
time: 1890 us; the launch traced here: 1880 us
  waiting for transfers between devices  916 us (48%)
  matrix products  494 us (26%)
  blocking collectives  204 us (11%)
  local copies, waits for them, and re-layouts  132 us (7%)
  other arithmetic  97.5 us (5%)
  starting transfers between devices  23.9 us (1%)
    unnamed x13, waiting for transfers between devices  158 us
    reduce_scatter x1, waiting for transfers between devices, shards(): lax.psum_scatter(query_wgrad, ('dp', 'expert'), scatter_dimension=0, tile...  141 us
    ppermute x7, waiting for transfers between devices, exchange_in_pairs(): done.append(lax.ppermute(sent, axis, [(i, i ^ turn) for i in range(peers)]))  137 us
    reduce_scatter x1, waiting for transfers between devices, shards(): lax.psum_scatter(pair_wgrad, ('dp', 'expert'), scatter_dimension=0, tiled...  121 us
    all_gather x1, blocking collectives, shards(): lax.all_gather(w_router, ('dp', 'expert'), axis=0, tiled=True)  121 us
    reduce_scatter x1, waiting for transfers between devices, shards(): lax.psum_scatter(gate_up_wgrads.astype(jnp.bfloat16), 'dp', scatter_dimen...  104 us
    sub x16, matrix products, head_probs(): exponent = jnp.exp(scores - largest)  95.5 us
    reduce_scatter x1, waiting for transfers between devices, shards(): lax.psum_scatter(out_wgrad, ('dp', 'expert'), scatter_dimension=1, tiled=...  89.3 us
  transfers between devices with their start and end apart: 21, of which 13 were waited for; matrix products, arithmetic and copies ran while one was open for 17% of the time, Pallas kernels for 0%

profile of v1, /device:TPU:0, one launch (start us, length us, event | category | flops | bytes accessed | tf_op | source)
XLA Modules:
  0.0 1882.8 jit_solution(4268014009549977786)
XLA Ops:
  10.4 42.1 %all-reduce.5 = (bf16[1536]{0:T(1024)(128)(2,1)S(1)}, bf16[1536]{0:T(1024)(128)(2,1)S(1)}) all-reduce(bf16[1536]{0:T(1024)(128)(2,1)S(1)} %dynamic-update-slice, bf16[1536]{0:T(1024)(128)(2,1)S(1)} %dynamic-update-slice.1), channel_id=1, replica_groups=mesh['dp'=4,'expert'=8] {'dp','expert'}, use_global_device_ids=true, to_apply=%add | all-reduce | flops 3072 | bytes 12288
  55.3 17.3 all-gather.6.cloned.1.call-done
  95.1 42.9 %all-gather.10.cloned.1.call-done = bf16[1536,1536]{1,0:T(8,128)(2,1)} async-done(((bf16[48,1536]{1,0:T(8,128)(2,1)}), bf16[1536,1536]{1,0:T(8,128)(2,1)}) %all-gather.10.cloned.1.call-update) | async-done | bytes 4718608 | tf_op jit(solution)/shard_map/all_gather | solution.py:104
  143.9 32.2 %all-gather.8.cloned.1.call-done = bf16[2048,1024]{1,0:T(8,128)(2,1)} async-done(((bf16[256,1024]{1,0:T(8,128)(2,1)}), bf16[2048,1024]{1,0:T(8,128)(2,1)}) %all-gather.8.cloned.1.call-update) | async-done | bytes 4194320 | tf_op jit(solution)/shard_map/all_gather | solution.py:137
  188.5 100.7 %while.28 = (s32[]{:T(128)}, bf16[8,256,3,64]{1,3,2,0:T(8,128)(2,1)}, bf16[8,2048,64]{1,2,0:T(8,128)(2,1)}, bf16[8,2048,64]{1,2,0:T(8,128)(2,1)}, bf16[8,256,3,6...) while((s32[]{:T(128)}, ...), condition=%wide.region_4.5_spmd.clone.clone, body=%wide.region_1.4_spmd.clone.sunk.clone | while | flops 413665280 | bytes 14477413 | solution.py:160
  295.8 15.0 scatter_custom_fusion
  315.8 120.7 %all-gather = bf16[32,48,16]{1,2,0:T(8,128)(2,1)S(1)} all-gather(bf16[1,48,16]{1,2,0:T(8,128)(2,1)S(1)} %bitcast.411), channel_id=1, replica_groups=mesh['dp'=4,'expert'=8] {'dp','expert'}, dimensions={0}, use_global_device_ids=true | all-gather | bytes 50688 | tf_op jit(solution)/shard_map/all_gather | solution.py:107
  441.1 15.8 scatter_custom_fusion.1
  461.8 15.0 fusion.142
  476.8 73.4 %all-to-all-done.1 = bf16[8,320,1536]{2,1,0:T(8,128)(2,1)} async-done(((bf16[8,320,1536]{2,1,0:T(8,128)(2,1)}), bf16[8,320,1536]{2,1,0:T(8,128)(2,1)}, u32[]{:S(2)}, u32[]{:S(2)}) %all-to-all-start.1) | async-done | bytes 7864352 | tf_op jit(solution)/shard_map/all_to_all | solution.py:211
  564.6 13.7 convert_bitcast_fusion
  621.0 78.3 %collective-permute-done.1 = bf16[1,320,1536]{2,1,0:T(8,128)(2,1)} collective-permute-done((bf16[1,320,1536]{2,1,0:T(8,128)(2,1)}, bf16[1,320,1536]{2,1,0:T(8,128)(2,1)}, u32[]{:S(2)}, u32[]{:S(2)}) %collective-permute-start.1) | collective-permute-done | bytes 983072 | tf_op jit(solution)/shard_map/ppermute | solution.py:39
  703.0 58.5 %collective-permute-done.2 = bf16[1,320,1536]{2,1,0:T(8,128)(2,1)S(1)} collective-permute-done((bf16[1,320,1536]{2,1,0:T(8,128)(2,1)}, bf16[1,320,1536]{2,1,0:T(8,128)(2,1)S(1)}, u32[]{:S(2)}, u32[]{:S(2)}) %collective-permute-start.2) | collective-permute-done | bytes 983072 | tf_op jit(solution)/shard_map/ppermute | solution.py:39
  774.7 17.6 gather_fusion.1
  801.9 17.7 gather_fusion.2
  833.4 306.4 %while.29 = (s32[]{:T(128)}, f32[8,256,3,64]{1,3,2,0:T(8,128)}, bf16[8,2048,64]{1,2,0:T(8,128)(2,1)}, bf16[8,2048,64]{1,2,0:T(8,128)(2,1)}, bf16[8,2048,64]{1,2,...) while((s32[]{:T(128)}, f32[8,256,3,64]{1,3,2,0:T(8,128)}, ...), condition=%wide.region_24.25_spmd.clone.clone, body=%wide.region_20.24_spmd.clone.sunk.clone | while | flops 1039670784 | bytes 72726648 | solution.py:284
  1166.9 13.9 bitcast_convert_fusion
  1199.7 95.5 %reduce-scatter.22.cloned.1.call-done = f32[48,16]{1,0:T(8,128)} async-done(((f32[1536,16]{1,0:T(8,128)}), f32[48,16]{1,0:T(8,128)}) %reduce-scatter.22.cloned.1.call-update) | async-done | bytes 3088
  1296.6 60.9 %reduce-scatter.24.cloned.1.call-done = bf16[384,1024]{1,0:T(8,128)(2,1)} async-done(((bf16[1536,1024]{1,0:T(8,128)(2,1)}), bf16[384,1024]{1,0:T(8,128)(2,1)}) %reduce-scatter.24.cloned.1.call-update) | async-done | bytes 786448
  1367.0 103.7 %reduce-scatter.20.cloned.1.call-done = bf16[2,384,1024]{2,1,0:T(8,128)(2,1)} async-done(((bf16[2,1536,1024]{2,1,0:T(8,128)(2,1)}), bf16[2,384,1024]{2,1,0:T(8,128)(2,1)}) %reduce-scatter.20.cloned.1.call-update) | async-done | bytes 1572880 | tf_op jit(solution)/shard_map/reduce_scatter | solution.py:319
  1479.4 40.9 %all-reduce.4 = (f32[1536]{0:T(1024)S(1)}, f32[1536]{0:T(1024)S(1)}) all-reduce(f32[1536]{0:T(1024)S(1)} %get-tuple-element.153, f32[1536]{0:T(1024)S(1)} %copy-done.30), channel_id=7, replica_groups=mesh['dp'=4,'expert'=8] {'dp','expert'}, use_global_device_ids=true, to_apply=%region_32.33.clone | all-reduce | flops 3072 | bytes 24576
  1524.9 89.3 %reduce-scatter.18.cloned.1.call-done = f32[1536,48]{0,1:T(8,128)} async-done(((f32[1536,1536]{0,1:T(8,128)}), f32[1536,48]{0,1:T(8,128)}) %reduce-scatter.18.cloned.1.call-update) | async-done | bytes 294928 | tf_op jit(solution)/shard_map/reduce_scatter | solution.py:313
  1614.2 140.9 %reduce-scatter.14.cloned.1.call-done = f32[48,1536]{1,0:T(8,128)} async-done(((f32[1536,1536]{1,0:T(8,128)}), f32[48,1536]{1,0:T(8,128)}) %reduce-scatter.14.cloned.1.call-update) | async-done | bytes 294928 | tf_op jit(solution)/shard_map/reduce_scatter | solution.py:311
  1755.1 120.9 %reduce-scatter.16.cloned.1.call-done = f32[48,1024]{1,0:T(8,128)} async-done(((f32[1536,1024]{1,0:T(8,128)}), f32[48,1024]{1,0:T(8,128)}) %reduce-scatter.16.cloned.1.call-update) | async-done | bytes 196624 | tf_op jit(solution)/shard_map/reduce_scatter | solution.py:312
  (300 shorter events, 641.3 us)
Async XLA Ops:
  7.2 543.0 %copy-start = (bf16[2,512,1536]{2,1,0:T(8,128)(2,1)S(1)}, bf16[2,512,1536]{2,1,0:T(8,128)(2,1)}, u32[]{:S(2)}) copy-start(bf16[2,512,1536]{2,1,0:T(8,128)(2,1)} %param.26) | copy-start | bytes 9437188
  7.2 65.4 %all-gather.6.cloned.1.call-start = ((), (), s32[]{:S(2)}) async-start(), calls=%async_computation.10 | async-start | bytes 3244032 | tf_op jit(solution)/shard_map/all_gather | solution.py:105
  7.9 130.1 %all-gather.10.cloned.1.call-start = ((), (), s32[]{:S(2)}) async-start(), calls=%async_computation.12 | async-start | bytes 4866048 | tf_op jit(solution)/shard_map/all_gather | solution.py:104
  8.7 167.4 %all-gather.8.cloned.1.call-start = ((), (), s32[]{:S(2)}) async-start(), calls=%async_computation.11 | async-start | bytes 4718592 | tf_op jit(solution)/shard_map/all_gather | solution.py:137
  55.3 87.4 %copy-start.18 = (f32[256,32]{0,1:T(8,128)}, f32[256,32]{0,1:T(8,128)S(1)}, u32[]{:S(2)}) copy-start(f32[256,32]{0,1:T(8,128)S(1)} %get-tuple-element.232) | copy-start | bytes 98308
  83.3 205.9 %all-gather.12.cloned.1.call-start = ((), (), s32[]{:S(2)}) async-start(), calls=%async_computation.13 | async-start | bytes 4866048 | tf_op jit(solution)/shard_map/all_gather | solution.py:106
  310.8 146.1 %all-to-all-start = ((bf16[8,320,1536]{2,1,0:T(8,128)(2,1)}), bf16[8,320,1536]{2,1,0:T(8,128)(2,1)}, u32[]{:S(2)}, u32[]{:S(2)}) async-start(bf16[8,320,1536]{2,1,0:T(8,128)(2,1)} %bitcast.382), calls=%async_computation | async-start | bytes 15728640 | tf_op jit(solution)/shard_map/all_to_all | solution.py:182
  456.9 93.4 %all-to-all-start.1 = ((bf16[8,320,1536]{2,1,0:T(8,128)(2,1)}), bf16[8,320,1536]{2,1,0:T(8,128)(2,1)}, u32[]{:S(2)}, u32[]{:S(2)}) async-start(bf16[8,320,1536]{2,1,0:T(8,128)(2,1)} %bitcast.381), calls=%async_computation.1 | async-start | bytes 15728640 | tf_op jit(solution)/shard_map/all_to_all | solution.py:211
  585.3 216.6 %all-to-all-start.2 = ((bf16[8,320,1536]{2,1,0:T(8,128)(2,1)}), bf16[8,320,1536]{2,1,0:T(8,128)(2,1)}, u32[]{:S(2)}, u32[]{:S(2)}) async-start(bf16[8,320,1536]{2,1,0:T(8,128)(2,1)} %bitcast.380), calls=%async_computation.2 | async-start | bytes 15728640 | tf_op jit(solution)/shard_map/all_to_all | solution.py:230
  590.2 604.3 %reduce-scatter.12.cloned.1.call-start = ((), (), s32[]{:S(2)}) async-start(), calls=%async_computation.14 | async-start | bytes 4718592 | tf_op jit(solution)/shard_map/reduce_scatter | solution.py:295
  612.1 6.2 collective-permute-start
  612.5 86.9 %collective-permute-start.1 = (bf16[1,320,1536]{2,1,0:T(8,128)(2,1)}, bf16[1,320,1536]{2,1,0:T(8,128)(2,1)}, u32[]{:S(2)}, u32[]{:S(2)}) collective-permute-start(bf16[1,320,1536]{2,1,0:T(8,128)(2,1)} %get-tuple-element.213), channel_id=1, source_target_pairs={{0,2},{1,3},{2,0},{3,1},{4,6},{5,7},{6,4},{7,5},{8,10},{9,11},{10,... | collective-permute-start | bytes 2949128 | tf_op jit(solution)/shard_map/ppermute | solution.py:39
  614.4 151.6 %collective-permute-start.6 = (bf16[1,320,1536]{2,1,0:T(8,128)(2,1)}, bf16[1,320,1536]{2,1,0:T(8,128)(2,1)S(1)}, u32[]{:S(2)}, u32[]{:S(2)}) collective-permute-start(bf16[1,320,1536]{2,1,0:T(8,128)(2,1)} %get-tuple-element.208), channel_id=1, source_target_pairs={{0,7},{1,6},{2,5},{3,4},{4,3},{5,2},{6,1},{7,0},{8,15},{9,14},{10,... | collective-permute-start | bytes 2949128 | tf_op jit(solution)/shard_map/ppermute | solution.py:39
  615.6 149.3 %collective-permute-start.5 = (bf16[1,320,1536]{2,1,0:T(8,128)(2,1)}, bf16[1,320,1536]{2,1,0:T(8,128)(2,1)S(1)}, u32[]{:S(2)}, u32[]{:S(2)}) collective-permute-start(bf16[1,320,1536]{2,1,0:T(8,128)(2,1)} %get-tuple-element.209), channel_id=1, source_target_pairs={{0,6},{1,7},{2,4},{3,5},{4,2},{5,3},{6,0},{7,1},{8,14},{9,15},{10,... | collective-permute-start | bytes 2949128 | tf_op jit(solution)/shard_map/ppermute | solution.py:39
  617.1 146.8 %collective-permute-start.4 = (bf16[1,320,1536]{2,1,0:T(8,128)(2,1)}, bf16[1,320,1536]{2,1,0:T(8,128)(2,1)S(1)}, u32[]{:S(2)}, u32[]{:S(2)}) collective-permute-start(bf16[1,320,1536]{2,1,0:T(8,128)(2,1)} %get-tuple-element.210), channel_id=1, source_target_pairs={{0,5},{1,4},{2,7},{3,6},{4,1},{5,0},{6,3},{7,2},{8,13},{9,12},{10,... | collective-permute-start | bytes 2949128 | tf_op jit(solution)/shard_map/ppermute | solution.py:39
  618.3 143.2 %collective-permute-start.2 = (bf16[1,320,1536]{2,1,0:T(8,128)(2,1)}, bf16[1,320,1536]{2,1,0:T(8,128)(2,1)S(1)}, u32[]{:S(2)}, u32[]{:S(2)}) collective-permute-start(bf16[1,320,1536]{2,1,0:T(8,128)(2,1)} %get-tuple-element.212), channel_id=1, source_target_pairs={{0,3},{1,2},{2,1},{3,0},{4,7},{5,6},{6,5},{7,4},{8,11},{9,10},{10,... | collective-permute-start | bytes 2949128 | tf_op jit(solution)/shard_map/ppermute | solution.py:39
  699.3 63.5 %collective-permute-start.3 = (bf16[1,320,1536]{2,1,0:T(8,128)(2,1)}, bf16[1,320,1536]{2,1,0:T(8,128)(2,1)S(1)}, u32[]{:S(2)}, u32[]{:S(2)}) collective-permute-start(bf16[1,320,1536]{2,1,0:T(8,128)(2,1)} %get-tuple-element.211), channel_id=1, source_target_pairs={{0,4},{1,5},{2,6},{3,7},{4,0},{5,1},{6,2},{7,3},{8,12},{9,13},{10,... | collective-permute-start | bytes 2949128 | tf_op jit(solution)/shard_map/ppermute | solution.py:39
  1144.7 150.5 %reduce-scatter.22.cloned.1.call-start = ((), (), s32[]{:S(2)}) async-start(), calls=%async_computation.19 | async-start | bytes 811008
  1146.1 211.4 %reduce-scatter.24.cloned.1.call-start = ((), (), s32[]{:S(2)}) async-start(), calls=%async_computation.20 | async-start | bytes 3932160
  1166.9 303.8 %reduce-scatter.20.cloned.1.call-start = ((), (), s32[]{:S(2)}) async-start(), calls=%async_computation.18 | async-start | bytes 7864320 | tf_op jit(solution)/shard_map/reduce_scatter | solution.py:319
  1180.9 433.3 %reduce-scatter.18.cloned.1.call-start = ((), (), s32[]{:S(2)}) async-start(), calls=%async_computation.17 | async-start | bytes 9732096 | tf_op jit(solution)/shard_map/reduce_scatter | solution.py:313
  1187.6 567.5 %reduce-scatter.14.cloned.1.call-start = ((), (), s32[]{:S(2)}) async-start(), calls=%async_computation.15 | async-start | bytes 9732096 | tf_op jit(solution)/shard_map/reduce_scatter | solution.py:311
  1194.5 681.5 %reduce-scatter.16.cloned.1.call-start = ((), (), s32[]{:S(2)}) async-start(), calls=%async_computation.16 | async-start | bytes 6488064 | tf_op jit(solution)/shard_map/reduce_scatter | solution.py:312
  1470.7 405.3 %copy-start.1 = (bf16[2,512,1536]{2,1,0:T(8,128)(2,1)S(1)}, bf16[2,512,1536]{2,1,0:T(8,128)(2,1)}, u32[]{:S(2)}) copy-start(bf16[2,512,1536]{2,1,0:T(8,128)(2,1)} %param.26) | copy-start | bytes 9437188
  (35 other events, 390.0 us)
Sparse Core Ops, SparseCore 0:
  10.9 61.6 all-gather.5
  75.5 62.4 all-gather.9
  140.5 35.5 all-gather.7
  178.8 63.6 all-gather.11
  1144.8 48.4 reduce-scatter.11
  1199.6 95.4 reduce-scatter.21
  1298.1 59.3 reduce-scatter.23
  1359.9 110.7 reduce-scatter.19
  1478.2 135.9 reduce-scatter.17
  1620.5 134.5 reduce-scatter.13
  1762.3 113.6 reduce-scatter.15
